TPU v7x, 256 devices: a whole 4x4x8 slice. The times are simulated.
256 devices in a mesh: energy: 8 (over y_hi, x), block: 32 (over y_lo, z, core).
Axes of the slice: x: 4, y: 4 (y_hi: 2, y_lo: 2; y = y_hi * 2 + y_lo), z: 8, core: 2. Of those that a mesh axis runs over, the one named last changes fastest.
Arguments:
- g_less: bfloat16 [256, 32, 128, 128], P('energy', 'block'), may hold values from -6 to 6
- g_great: bfloat16 [256, 32, 128, 128], P('energy', 'block'), may hold values from -6 to 6
- coupling: bfloat16 [32, 3, 128, 128], P('block'), may hold values from -0.3125 to 0.3125
- coupling_mask: int32 [32, 2], P('block'), may hold values 0 or 1
Outputs:
- sigma_less: float32 [256, 32, 128, 128], P('energy', 'block')
All inputs are finite; a program needn't handle non-finite values. No bound on the sum of `coupling_mask` on one device may be relied on, other than what follows from the above.
Results may differ from a plain program's by a relative error of at most 0.009.
Values may be sent and summed in bfloat16 or wider, within the bound.
A program may use at most 64 MiB of HBM per device.

v0:
```python
import math

import jax
import jax.numpy as jnp
from jax import lax
from jax.sharding import PartitionSpec as P


def sent_together(arrays, axis, split_dim, concat_dim, along):
    widths = [a.shape[along] for a in arrays]
    both = jnp.concatenate(arrays, axis=along)
    filled = lax.all_to_all(both, axis, split_axis=split_dim, concat_axis=concat_dim, tiled=True)
    return tuple(jnp.split(filled, [sum(widths[:k]) for k in range(1, len(widths))], axis=along))


def padded(array, sides, width):
    for axis, dim in sides:
        peers, length = (lax.axis_size(axis), array.shape[dim])
        up = [(i, (i + 1) % peers) for i in range(peers - 1)]
        down = [(j, i) for i, j in up]
        last = lax.slice_in_dim(array, length - width, length, axis=dim)
        leading = lax.slice_in_dim(array, 0, width, axis=dim)
        before = lax.ppermute(last, axis, up)
        after = lax.ppermute(leading, axis, down)
        array = jnp.concatenate([before, array, after], axis=dim)
    return array


def cut_along(array, dim, peers):
    before, after = (array.shape[:dim], array.shape[dim + 1 :])
    return jnp.moveaxis(array.reshape(*before, peers, -1, *after), dim, 0)


def edges_of(length, count):
    lap = length // count
    if lap >= 8:
        lap -= lap % 8
    return [lap * k for k in range(1, count)]


def laid_out(parts, dim):
    lengths = list(parts.shape[1:])
    lengths[dim] *= parts.shape[0]
    return jnp.moveaxis(parts, 0, dim).reshape(lengths)


def cut_exchange(array, axis, pieces, split_dim, concat_dim):
    parts = cut_along(array, split_dim, lax.axis_size(axis))
    cut = max(range(1, max(2, parts.ndim - 1)), key=lambda d: parts.shape[d])
    done = []
    for share in jnp.split(parts, edges_of(parts.shape[cut], pieces), axis=cut):
        if share.size:
            done.append(lax.all_to_all(share, axis, split_axis=0, concat_axis=0, tiled=True))
    return laid_out(jnp.concatenate(done, axis=cut), concat_dim)


def angle_table(row_index, col_index, length):
    turns = row_index[:, None] * col_index[None, :] % length
    theta = turns.astype(jnp.float32) * (2.0 * math.pi / length)
    return (jnp.cos(theta), jnp.sin(theta))


def product(table, values):
    return jnp.dot(
        table, values, precision=lax.Precision.HIGHEST, preferred_element_type=jnp.float32
    )


def split_product(table, values):
    upper = table.astype(jnp.bfloat16)
    lower = (table - upper.astype(jnp.float32)).astype(jnp.bfloat16)
    first = jnp.dot(upper, values, preferred_element_type=jnp.float32)
    return first + jnp.dot(lower, values, preferred_element_type=jnp.float32)


def shards(g_less, g_great, coupling, coupling_mask):
    e_dev, blocks, orbitals, _ = g_less.shape
    groups = lax.axis_size("energy")
    total_e = e_dev * groups
    length = 2 * total_e
    element_count = orbitals * orbitals // groups
    highest = lax.Precision.HIGHEST
    less_flat = g_less.reshape(e_dev, blocks, orbitals * orbitals)
    great_turned = jnp.swapaxes(g_great, 2, 3).reshape(e_dev, blocks, orbitals * orbitals)
    less_group, great_group = sent_together((less_flat, great_turned), "energy", 2, 0, 1)
    frequency = jnp.arange(total_e + 1, dtype=jnp.int32)
    energies = jnp.arange(total_e, dtype=jnp.int32)
    lag_index = energies - total_e // 2
    cos_fwd, sin_fwd = angle_table(frequency, energies, length)
    cos_lag, sin_lag = angle_table(lag_index, frequency, length)
    inner = (frequency > 0) & (frequency < total_e)
    weight = jnp.where(inner, 2.0, 1.0).astype(jnp.float32)
    factor = 1.0 / (length * math.sqrt(total_e))
    less_data = less_group.reshape(total_e, blocks * element_count)
    great_data = great_group.reshape(total_e, blocks * element_count)
    less_cos = split_product(cos_fwd, less_data)
    less_sin = split_product(sin_fwd, less_data)
    great_cos = split_product(cos_fwd, great_data)
    great_sin = split_product(sin_fwd, great_data)
    real_part = less_cos * great_cos + less_sin * great_sin
    imag_part = less_cos * great_sin - less_sin * great_cos
    pol = (
        product(cos_lag * weight[None, :], real_part)
        - product(sin_lag * weight[None, :], imag_part)
    ) * factor
    pol_back = lax.all_to_all(
        pol.reshape(total_e, blocks, element_count),
        "energy",
        split_axis=0,
        concat_axis=2,
        tiled=True,
    )
    pol_back = pol_back.reshape(e_dev, blocks, orbitals, orbitals)
    pol_padded = padded(pol_back, (("block", 1),), 1)
    present = coupling_mask.astype(jnp.float32)
    weights = jnp.stack([present[:, 0], jnp.ones((blocks,), jnp.float32), present[:, 1]], axis=1)
    coupled = coupling.astype(jnp.float32)
    shifted = [pol_padded[:, offset : offset + blocks] for offset in range(3)]
    screened = jnp.zeros((e_dev, blocks, orbitals, orbitals), jnp.float32)
    for offset in range(3):
        halfway = jnp.einsum(
            "bij,ebjk->ebik", coupled[:, offset], shifted[offset], precision=highest
        )
        term = jnp.einsum("ebik,blk->ebil", halfway, coupled[:, offset], precision=highest)
        screened = screened + weights[None, :, offset, None, None] * term
    screened_flat = screened.astype(jnp.bfloat16).reshape(e_dev, blocks, orbitals * orbitals)
    screened_group = cut_exchange(screened_flat, "energy", 2, 2, 0)
    inter_data = screened_group.reshape(total_e, blocks * element_count)
    inter_cos = split_product(cos_lag.T, inter_data)
    inter_sin = split_product(sin_lag.T, inter_data)
    sum_real = less_cos * inter_cos - less_sin * inter_sin
    sum_imag = less_cos * inter_sin + less_sin * inter_cos
    back_cos = (cos_fwd * weight[:, None]).T
    back_sin = (sin_fwd * weight[:, None]).T
    sigma = (product(back_cos, sum_real) + product(back_sin, sum_imag)) * factor
    sigma_back = lax.all_to_all(
        sigma.reshape(total_e, blocks, element_count),
        "energy",
        split_axis=0,
        concat_axis=2,
        tiled=True,
    )
    return sigma_back.reshape(e_dev, blocks, orbitals, orbitals)


def solution(mesh):
    return jax.shard_map(
        shards,
        mesh=mesh,
        in_specs=(
            P("energy", "block", None, None),
            P("energy", "block", None, None),
            P("block", None, None, None),
            P("block", None),
        ),
        out_specs=P("energy", "block", None, None),
        check_vma=False,
    )
```

profile of v0, /device:TPU:128, one launch (start us, length us, event | category | flops | bytes accessed | tf_op | source)
XLA Modules:
  0.0 278.0 jit_solution(18001592523919180427)
XLA Ops:
  4.9 12.9 %copy.36 = bf16[32,2,16384]{0,1,2:T(2,128)(2,1)} copy(bf16[32,2,16384]{2,0,1:T(8,128)(2,1)S(1)} %pad_maximum_fusion) | data formatting | bytes 4194304 | tf_op jit(solution)/shard_map/concatenate | solution.py:11
  17.8 11.2 %reshape.122 = bf16[8,2,65536]{2,1,0:T(2,128)(2,1)} reshape(bf16[16384,2,32]{2,1,0:T(2,128)(2,1)} %bitcast.132) | data formatting | bytes 4194304
  29.0 6.9 %all-to-all-start = ((bf16[8,2,65536]{2,1,0:T(2,128)(2,1)}), bf16[8,2,65536]{2,1,0:T(2,128)(2,1)S(1)}, u32[]{:S(2)}, u32[]{:S(2)}) async-start(bf16[8,2,65536]{2,1,0:T(2,128)(2,1)} %reshape.122), calls=%async_computation | async-start | bytes 4194304 | tf_op jit(solution)/shard_map/all_to_all | solution.py:12
  35.9 28.4 %all-to-all-done = bf16[8,2,65536]{2,1,0:T(2,128)(2,1)S(1)} async-done(((bf16[8,2,65536]{2,1,0:T(2,128)(2,1)}), bf16[8,2,65536]{2,1,0:T(2,128)(2,1)S(1)}, u32[]{:S(2)}, u32[]{:S(2)}) %all-to-all-start) | async-done | bytes 2097184 | tf_op jit(solution)/shard_map/all_to_all | solution.py:12
  64.4 6.5 %reshape.123 = bf16[16384,2,32]{2,1,0:T(2,128)(2,1)} reshape(bf16[8,2,65536]{2,1,0:T(2,128)(2,1)S(1)} %all-to-all-done) | data formatting | bytes 4194304
  70.9 18.3 %copy.57 = bf16[32,2,8,2048]{3,0,2,1:T(8,128)(2,1)S(1)} copy(bf16[32,2,8,2048]{0,1,3,2:T(2,128)(2,1)} %bitcast.133) | data formatting | bytes 4194304 | tf_op jit(solution)/shard_map/all_to_all | solution.py:12
  94.8 2.8 convolution_add_fusion.5
  101.8 5.4 %fusion.14 = f32[256,2048]{1,0:T(8,128)S(1)} fusion(f32[257,2048]{1,0:T(8,128)S(1)} %convolution_add_fusion.3, f32[257,2048]{1,0:T(8,128)S(1)} %convolution_add_fusion.2, f32[257,2048]{1,0:T(8,128)S(1)} %convolution_add_fusion.5, f32[257,2048]{1,0:T(8,128)S(1)} %convolution_add_fusion.4, f32[257]{0:T(512)S(1)} %fusion.103, s32[256]{0:T(256)S(1)} %iota_add_fusion), kind=kOutput, calls=%fused_computation.22 | convolution fusion | flops 1619470080 | bytes 10520580 | tf_op jit(solution)/shard_map/dot_general | solution.py:64
  107.2 5.3 %fusion.3 = f32[256,1,2048]{2,0,1:T(8,128)S(1)} fusion(f32[256,2048]{1,0:T(8,128)S(1)} %fusion.14, f32[257,2048]{1,0:T(8,128)S(1)} %convolution_add_fusion.3, f32[257,2048]{1,0:T(8,128)S(1)} %convolution_add_fusion.4, f32[257,2048]{1,0:T(8,128)S(1)} %convolution_add_fusion.5, f32[257,2048]{1,0:T(8,128)S(1)} %convolution_add_fusion.2, f32[257]{0:T(512)S(1)} %fusion.103, ...), kind=kOutput, calls=%fused_computation.11 | convolution fusion | flops 1620518656 | bytes 12617732 | tf_op jit(solution)/shard_map/dot_general | solution.py:64
  114.8 33.1 %all_to_all.58 = f32[256,1,2048]{2,1,0:T(1,128)S(1)} all-to-all(f32[256,1,2048]{2,1,0:T(1,128)S(1)} %copy.39), channel_id=1, replica_groups=mesh['energy'=8,'block'=32] {'energy'}, dimensions={0} | all-to-all | bytes 4194304 | tf_op jit(solution)/shard_map/all_to_all | solution.py:106
  147.9 2.5 copy.60
  150.4 2.7 reshape.107
  153.2 2.9 %copy.41 = f32[32,1,128,128]{2,3,0,1:T(8,128)} copy(f32[32,1,128,128]{3,2,0,1:T(8,128)} %reshape.107) | data formatting | bytes 4194304 | tf_op jit(solution)/shard_map/reshape | solution.py:113
  161.1 2.9 %reshape.111 = f32[32,128,128]{2,1,0:T(8,128)} reshape(f32[32,1,8,2048]{3,2,0,1:T(8,128)} %bitcast.139) | data formatting | bytes 4194304 | tf_op jit(solution)/shard_map/reshape.16
  164.0 3.4 %fusion.92 = f32[32,128,128]{2,1,0:T(8,128)S(1)} fusion(f32[32,128,128]{2,1,0:T(8,128)} %reshape.111, bf16[1,3,128,128]{3,2,1,0:T(8,128)(2,1)S(1)} %copy-done.5), kind=kOutput, calls=%fused_computation.102 | convolution fusion | flops 805306368 | bytes 4227072 | tf_op jit(solution)/shard_map/bij,ebjk->ebik/dot_general | solution.py:121
  169.3 12.6 %collective-permute-done.1 = f32[32,1,128,128]{2,3,0,1:T(8,128)} collective-permute-done((f32[32,1,128,128]{2,3,0,1:T(8,128)}, f32[32,1,128,128]{2,3,0,1:T(8,128)}, u32[]{:S(2)}, u32[]{:S(2)}) %collective-permute-start.1) | collective-permute-done | bytes 2097184 | tf_op jit(solution)/shard_map/ppermute | solution.py:24
  181.9 2.7 fusion.24
  186.9 2.7 fusion.26
  189.6 4.3 %fusion.30 = bf16[32,1,128,128]{3,2,0,1:T(8,128)(2,1)} fusion(f32[32,128,128]{2,1,0:T(8,128)S(1)} %fusion.18, f32[32,128,128]{2,1,0:T(8,128)S(1)} %fusion.20, f32[32,128,128]{2,1,0:T(8,128)S(1)} %fusion.26, f32[]{:T(128)} %bitcast.23, f32[]{:T(128)} %bitcast.6, bf16[1,3,128,128]{3,2,1,0:T(8,128)(2,1)S(1)} %copy-done.5), kind=kOutput, calls=%fused_computation.39 | convolution fusion | flops 807927808 | bytes 7372808 | tf_op jit(solution)/shard_map/ebik,blk->ebil/dot_general | solution.py:124
  196.0 15.5 %all_to_all.59 = bf16[8,16,1,2048]{3,1,2,0:T(8,128)(2,1)S(1)} all-to-all(bf16[8,16,1,2048]{3,1,2,0:T(8,128)(2,1)S(1)} %get-tuple-element.5), channel_id=1, replica_groups=mesh['energy'=8,'block'=32] {'energy'}, dimensions={0} | all-to-all | bytes 1048576 | tf_op jit(solution)/shard_map/all_to_all | solution.py:53
  211.6 14.5 %all_to_all.60 = bf16[8,16,1,2048]{3,1,2,0:T(8,128)(2,1)S(1)} all-to-all(bf16[8,16,1,2048]{3,1,2,0:T(8,128)(2,1)S(1)} %get-tuple-element.6), channel_id=1, replica_groups=mesh['energy'=8,'block'=32] {'energy'}, dimensions={0} | all-to-all | bytes 1048576 | tf_op jit(solution)/shard_map/all_to_all | solution.py:53
  232.0 4.8 %fusion.7 = f32[256,2048]{1,0:T(8,128)S(1)} fusion(f32[257,2048]{1,0:T(8,128)S(1)} %copy-done.1, f32[257,2048]{1,0:T(8,128)S(1)} %convolution_add_fusion, f32[257,2048]{1,0:T(8,128)S(1)} %convolution_add_fusion.5, f32[257,2048]{1,0:T(8,128)S(1)} %convolution_add_fusion.1, f32[257]{0:T(512)S(1)} %fusion.103), kind=kOutput, calls=%fused_computation.15 | convolution fusion | flops 1619470080 | bytes 10519556 | tf_op jit(solution)/shard_map/dot_general | solution.py:64
  236.8 5.1 %fusion.1 = f32[256,1,2048]{2,0,1:T(8,128)S(1)} fusion(f32[256,2048]{1,0:T(8,128)S(1)} %fusion.7, f32[257,2048]{1,0:T(8,128)S(1)} %copy-done.1, f32[257,2048]{1,0:T(8,128)S(1)} %convolution_add_fusion.1, f32[257,2048]{1,0:T(8,128)S(1)} %convolution_add_fusion.5, f32[257,2048]{1,0:T(8,128)S(1)} %convolution_add_fusion, f32[257]{0:T(512)S(1)} %fusion.103), kind=kOutput, calls=%fused_computation.8 | convolution fusion | flops 1620518656 | bytes 12616708 | tf_op jit(solution)/shard_map/dot_general | solution.py:64
  244.0 31.0 %all_to_all.61 = f32[256,1,2048]{2,1,0:T(1,128)S(1)} all-to-all(f32[256,1,2048]{2,1,0:T(1,128)S(1)} %copy.50), channel_id=1, replica_groups=mesh['energy'=8,'block'=32] {'energy'}, dimensions={0} | all-to-all | bytes 4194304 | tf_op jit(solution)/shard_map/all_to_all | solution.py:136
  (46 shorter events, 38.9 us)
Async XLA Ops:
  0.0 2.2 copy-start.4
  29.0 35.4 %all-to-all-start = ((bf16[8,2,65536]{2,1,0:T(2,128)(2,1)}), bf16[8,2,65536]{2,1,0:T(2,128)(2,1)S(1)}, u32[]{:S(2)}, u32[]{:S(2)}) async-start(bf16[8,2,65536]{2,1,0:T(2,128)(2,1)} %reshape.122), calls=%async_computation | async-start | bytes 4194304 | tf_op jit(solution)/shard_map/all_to_all | solution.py:12
  89.2 4.2 %copy-start.2 = (bf16[32,2,8,2048]{3,0,2,1:T(8,128)(2,1)}, bf16[32,2,8,2048]{3,0,2,1:T(8,128)(2,1)S(1)}, u32[]{:S(2)}) copy-start(bf16[32,2,8,2048]{3,0,2,1:T(8,128)(2,1)S(1)} %copy.57) | copy-start | bytes 6291460
  94.8 2.8 %copy-start.3 = (bf16[32,2,8,2048]{3,0,2,1:T(8,128)(2,1)S(1)}, bf16[32,2,8,2048]{3,0,2,1:T(8,128)(2,1)}, u32[]{:S(2)}) copy-start(bf16[32,2,8,2048]{3,0,2,1:T(8,128)(2,1)} %copy-done.2) | copy-start | bytes 6291460
  99.0 8.3 %copy-start = (f32[257,2048]{1,0:T(8,128)}, f32[257,2048]{1,0:T(8,128)S(1)}, u32[]{:S(2)}) copy-start(f32[257,2048]{1,0:T(8,128)S(1)} %convolution_add_fusion.3) | copy-start | bytes 6316036
  153.2 7.3 %copy-start.6 = (s32[1,2]{1,0:T(1,128)S(1)}, s32[1,2]{1,0:T(1,128)}, u32[]{:S(2)}) copy-start(s32[1,2]{1,0:T(1,128)} %param.7) | copy-start | bytes 28
  156.1 25.8 %collective-permute-start.1 = (f32[32,1,128,128]{2,3,0,1:T(8,128)}, f32[32,1,128,128]{2,3,0,1:T(8,128)}, u32[]{:S(2)}, u32[]{:S(2)}) collective-permute-start(f32[32,1,128,128]{2,3,0,1:T(8,128)} %copy.41), channel_id=1, source_target_pairs={{1,0},{2,1},{3,2},{4,3},{5,4},{6,5},{7,6},{8,7},{9,8},{10,9},{11,1... | collective-permute-start | bytes 6291464 | tf_op jit(solution)/shard_map/ppermute | solution.py:24
  158.0 28.9 %collective-permute-start = (f32[32,1,128,128]{2,3,0,1:T(8,128)}, f32[32,1,128,128]{2,3,0,1:T(8,128)}, u32[]{:S(2)}, u32[]{:S(2)}) collective-permute-start(f32[32,1,128,128]{2,3,0,1:T(8,128)} %copy.41), channel_id=1, source_target_pairs={{0,1},{1,2},{2,3},{3,4},{4,5},{5,6},{6,7},{7,8},{8,9},{9,10},{10,1... | collective-permute-start | bytes 6291464 | tf_op jit(solution)/shard_map/ppermute | solution.py:23
  161.1 3.0 %copy-start.5 = (bf16[1,3,128,128]{3,2,1,0:T(8,128)(2,1)S(1)}, bf16[1,3,128,128]{3,2,1,0:T(8,128)(2,1)}, u32[]{:S(2)}) copy-start(bf16[1,3,128,128]{3,2,1,0:T(8,128)(2,1)} %param.6) | copy-start | bytes 294916
  230.4 1.6 copy-start.1
where the time goes:
time: 282 us; the launch traced here: 278 us
  blocking collectives  94.2 us (33%)
  local copies, waits for them, and re-layouts  73.6 us (26%)
  matrix products  55.4 us (20%)
  waiting for transfers between devices  41.5 us (15%)
  starting transfers between devices  11.2 us (4%)
    all_to_all x1, blocking collectives, shards(): lax.all_to_all(pol.reshape(total_e, blocks, element_count), 'energy', spl...  33.1 us
    all_to_all x1, blocking collectives, shards(): lax.all_to_all(sigma.reshape(total_e, blocks, element_count), 'energy', s...  31 us
    all_to_all x2, blocking collectives, cut_exchange(): lax.all_to_all(share, axis, split_axis=0, concat_axis=0, tiled=True)  30 us
    all_to_all x1, waiting for transfers between devices, sent_together(): lax.all_to_all(both, axis, split_axis=split_dim, concat_axis=concat_dim,...  28.4 us
    dot_general x4, matrix products, product(): jnp.dot(table, values, precision=lax.Precision.HIGHEST, preferred_element...  20.7 us
    all_to_all x1, local copies, waits for them, and re-layouts, sent_together(): lax.all_to_all(both, axis, split_axis=split_dim, concat_axis=concat_dim,...  18.3 us
    unnamed x16, local copies, waits for them, and re-layouts  17.9 us
    concatenate x1, local copies, waits for them, and re-layouts, sent_together(): both = jnp.concatenate(arrays, axis=along)  12.9 us
  transfers between devices with their start and end apart: 3, of which 3 were waited for; matrix products, arithmetic and copies ran while one was open for 5% of the time, Pallas kernels for 0%

commit v1 on v0

v1 whole, which is shorter than its diff:
```python
import functools
import math

import jax
import jax.numpy as jnp
import numpy as np
from jax import lax
from jax.experimental import pallas as pl
from jax.experimental.pallas import tpu as pltpu
from jax.sharding import PartitionSpec as P

MESH = pl.DeviceIdType.MESH
F32, BF16 = jnp.float32, jnp.bfloat16

GROUPS = 8
ORB = 128
NE = 256
ROWS = ORB // GROUPS
SHARE = NE // GROUPS
HALF = SHARE // 2
PERIOD = NE + NE // 2
FREQ = PERIOD // 2
CHUNKS = 4
PER = ROWS // CHUNKS
PAIRS = ROWS // 2


def tables():
    freq = 2 * np.arange(FREQ) + 1
    result = []
    for points in (np.arange(NE), np.arange(NE) - NE // 2):
        angle = np.pi * ((freq[:, None] * points[None, :]) % (2 * PERIOD)) / PERIOD
        whole = np.concatenate([np.cos(angle), np.sin(angle)], axis=0).astype(np.float32)
        upper = whole.astype(jnp.bfloat16)
        lower = (whole - upper.astype(np.float32)).astype(jnp.bfloat16)
        result.append(np.stack([upper, lower]))
    return result


def swap_matrix():
    row = np.arange(ROWS * ROWS)
    return (row[None, :] == ((row % ROWS) * ROWS + row // ROWS)[:, None]).astype(jnp.bfloat16)


def offset_of(k):
    return (3 * k) % GROUPS


def peer(me, k, sign):
    step = offset_of(k)
    x = (me + sign * (step % 4) + 4) % 4
    y = (me // 4 + step // 4) % 2
    return y * 4 + x


def dot(a, b):
    return jnp.dot(a, b, preferred_element_type=F32)


def side_by_side(a, b):
    return jnp.concatenate([a, b], axis=1)


def kernel(
    less_hbm, great_hbm, coupling_ref, mask_ref, fwd_e_hbm, fwd_l_hbm, inv_l_hbm, inv_e_hbm, swap_hbm,
    out_hbm,
    less, great, fwd_e, fwd_l, inv_l, inv_e, swap,
    less_out, great_out, less_in, great_in, spec, pol, pol_out, pol_in, near, turned, half, scr, scr_out, scr_in, sig, sig_out, sig_in,
    load_sem, store_sem,
    less_s, less_r, great_s, great_r, pol_s, pol_r, near_s, near_r, scr_s, scr_r, sig_s, sig_r,
):
    me = lax.axis_index("energy")
    block = lax.axis_index("block")
    n_blocks = lax.axis_size("block")
    has_before, has_after = block > 0, block < n_blocks - 1

    loads = [
        pltpu.make_async_copy(src, dst, load_sem.at[k])
        for k, (src, dst) in enumerate(
            [(less_hbm.at[:, 0], less), (swap_hbm, swap), (great_hbm.at[:, 0], great), (fwd_e_hbm, fwd_e),
             (inv_l_hbm, inv_l), (fwd_l_hbm, fwd_l), (inv_e_hbm, inv_e)]
        )
    ]
    for load in loads:
        load.start()

    barrier = pltpu.get_barrier_semaphore()
    for k in range(1, GROUPS):
        pl.semaphore_signal(barrier, inc=1, device_id={"energy": peer(me, k, 1)}, device_id_type=MESH)

    @pl.when(has_before)
    def _():
        pl.semaphore_signal(barrier, inc=1, device_id={"block": block - 1}, device_id_type=MESH)

    @pl.when(has_after)
    def _():
        pl.semaphore_signal(barrier, inc=1, device_id={"block": block + 1}, device_id_type=MESH)

    def exchange(first, second):
        both = dot(swap[...], side_by_side(first, second)).astype(BF16)
        return both[:, :ORB].reshape(ROWS, ROWS, ORB), both[:, ORB:].reshape(ROWS, ROWS, ORB)

    def rows_of(k):
        return pl.ds(pl.multiple_of(peer(me, k, 1) * ROWS, ROWS), ROWS)

    def share_of(k):
        return pl.multiple_of(peer(me, k, 1) * SHARE, SHARE)

    my_rows = pl.ds(pl.multiple_of(me * ROWS, ROWS), ROWS)
    my_share = pl.multiple_of(me * SHARE, SHARE)

    def by_rows(source, k):
        rows = rows_of(k)
        return exchange(
            source[0:HALF, rows, :].reshape(ROWS * ROWS, ORB),
            source[HALF:SHARE, rows, :].reshape(ROWS * ROWS, ORB),
        )

    loads[0].wait()
    loads[1].wait()
    low, high = by_rows(less, 0)
    less_in[:, pl.ds(my_share, HALF), :] = low
    less_in[:, pl.ds(my_share + HALF, HALF), :] = high

    def less_step(k, carry):
        low, high = by_rows(less, k)
        less_out[k, :, 0:HALF, :] = low
        less_out[k, :, HALF:SHARE, :] = high
        return carry

    lax.fori_loop(1, GROUPS, less_step, 0)

    pl.semaphore_wait(barrier, GROUPS - 1 + has_before.astype(jnp.int32) + has_after.astype(jnp.int32))

    def less_copy(k):
        return pltpu.make_async_remote_copy(
            src_ref=less_out.at[k], dst_ref=less_in.at[:, pl.ds(my_share, SHARE), :],
            send_sem=less_s.at[k], recv_sem=less_r.at[k],
            device_id={"energy": peer(me, k, 1)}, device_id_type=MESH,
        )

    for k in range(1, GROUPS):
        less_copy(k).start()

    loads[2].wait()

    def turn_step(m, carry):
        turned[m] = great[m].T
        return carry

    lax.fori_loop(0, SHARE, turn_step, 0, unroll=2)
    low, high = by_rows(turned, 0)
    great_in[:, pl.ds(my_share, HALF), :] = low
    great_in[:, pl.ds(my_share + HALF, HALF), :] = high

    def great_step(k, carry):
        low, high = by_rows(turned, k)
        great_out[k, :, 0:HALF, :] = low
        great_out[k, :, HALF:SHARE, :] = high
        return carry

    lax.fori_loop(1, GROUPS, great_step, 0)

    def great_copy(c, k):
        rows = pl.ds(c * PER, PER)
        return pltpu.make_async_remote_copy(
            src_ref=great_out.at[k, rows], dst_ref=great_in.at[rows, pl.ds(my_share, SHARE), :],
            send_sem=great_s.at[c, k], recv_sem=great_r.at[c, k],
            device_id={"energy": peer(me, k, 1)}, device_id_type=MESH,
        )

    for c in range(CHUNKS):
        for k in range(1, GROUPS):
            great_copy(c, k).start()

    for load in loads[3:]:
        load.wait()

    for k in range(1, GROUPS):
        less_copy(k).wait_recv()

    def forward(table, source, p):
        pair = side_by_side(source[2 * p], source[2 * p + 1])
        return dot(table[0], pair) + dot(table[1], pair)

    def less_transform(p, carry):
        spec[p] = forward(fwd_e, less_in, p)
        return carry

    lax.fori_loop(0, PAIRS, less_transform, 0)

    scale = 1.0 / (FREQ * math.sqrt(NE))

    def backward(table, real, imag, p, result):
        both = jnp.concatenate([real.astype(BF16), imag.astype(BF16)], axis=0)
        value = ((dot(table[0], both) + dot(table[1], both)) * scale).astype(BF16)
        result[2 * p] = value[:, :ORB]
        result[2 * p + 1] = value[:, ORB:]

    def pol_step(p, carry):
        great_spec = forward(fwd_e, great_in, p)
        a_cos, a_sin = spec[p, :FREQ, :], spec[p, FREQ:, :]
        b_cos, b_sin = great_spec[:FREQ], great_spec[FREQ:]
        backward(inv_l, a_cos * b_cos + a_sin * b_sin, a_sin * b_cos - a_cos * b_sin, p, pol)
        return carry

    for c in range(CHUNKS):
        for k in range(1, GROUPS):
            great_copy(c, k).wait_recv()
        lax.fori_loop(c * PAIRS // CHUNKS, (c + 1) * PAIRS // CHUNKS, pol_step, 0)

    def to_share(source, k):
        first = share_of(k)
        return exchange(
            source[:, pl.ds(first, HALF), :].reshape(ROWS * ROWS, ORB),
            source[:, pl.ds(first + HALF, HALF), :].reshape(ROWS * ROWS, ORB),
        )

    low, high = to_share(pol, 0)
    pol_in[0, :, my_rows, :] = low
    pol_in[1, :, my_rows, :] = high

    def pol_out_step(k, carry):
        low, high = to_share(pol, k)
        pol_out[0, k] = low
        pol_out[1, k] = high
        return carry

    lax.fori_loop(1, GROUPS, pol_out_step, 0)

    def pol_copy(h, k):
        return pltpu.make_async_remote_copy(
            src_ref=pol_out.at[h, k], dst_ref=pol_in.at[h, :, my_rows, :],
            send_sem=pol_s.at[h, k], recv_sem=pol_r.at[h, k],
            device_id={"energy": peer(me, k, 1)}, device_id_type=MESH,
        )

    for h in range(2):
        for k in range(1, GROUPS):
            pol_copy(h, k).start()

    def near_copy(h, side, k):
        rows = pl.ds(pl.multiple_of(peer(me, k, -1) * ROWS, ROWS), ROWS)
        return pltpu.make_async_remote_copy(
            src_ref=pol_in.at[h, :, rows, :], dst_ref=near.at[h, side, :, rows, :],
            send_sem=near_s.at[h, side, k], recv_sem=near_r.at[h, side, k],
            device_id={"block": block + 1 - 2 * side}, device_id_type=MESH,
        )

    @pl.when(jnp.logical_not(has_before))
    def _():
        near[:, 0] = jnp.zeros((2, HALF, ORB, ORB), BF16)

    @pl.when(jnp.logical_not(has_after))
    def _():
        near[:, 1] = jnp.zeros((2, HALF, ORB, ORB), BF16)

    def scaled(t, factor):
        return (coupling_ref[0, t].astype(F32) * factor).astype(BF16)

    weights = [
        scaled(0, mask_ref[0, 0].astype(F32)), coupling_ref[0, 1], scaled(2, mask_ref[0, 1].astype(F32)),
    ]

    def halfway(h, t):
        def step(p, carry):
            if t == 1:
                pair = side_by_side(pol_in[h, 2 * p], pol_in[h, 2 * p + 1])
            else:
                pair = side_by_side(near[h, t // 2, 2 * p], near[h, t // 2, 2 * p + 1])
            value = dot(weights[t], pair).astype(BF16)
            half[t, 2 * p] = value[:, :ORB]
            half[t, 2 * p + 1] = value[:, ORB:]
            return carry

        lax.fori_loop(0, HALF // 2, step, 0)

    across = jnp.concatenate([coupling_ref[0, t].T for t in range(3)], axis=0)

    def scr_copy(h, k):
        return pltpu.make_async_remote_copy(
            src_ref=scr_out.at[h, k], dst_ref=scr_in.at[:, pl.ds(my_share + h * HALF, HALF), :],
            send_sem=scr_s.at[h, k], recv_sem=scr_r.at[h, k],
            device_id={"energy": peer(me, k, 1)}, device_id_type=MESH,
        )

    for h in range(2):
        for k in range(GROUPS):
            if k > 0:
                pol_copy(h, k).wait_recv()

            @pl.when(has_after)
            def _():
                near_copy(h, 0, k).start()

            @pl.when(has_before)
            def _():
                near_copy(h, 1, k).start()

        halfway(h, 1)

        @pl.when(has_before)
        def _():
            for k in range(GROUPS):
                near_copy(h, 0, k).wait_recv()

        halfway(h, 0)

        @pl.when(has_after)
        def _():
            for k in range(GROUPS):
                near_copy(h, 1, k).wait_recv()

        halfway(h, 2)

        def scr_step(p, carry):
            both = jnp.concatenate(
                [half[t, pl.ds(2 * p, 2)].reshape(2 * ORB, ORB) for t in range(3)], axis=1
            )
            scr[pl.ds(2 * p, 2)] = dot(both, across).astype(BF16).reshape(2, ORB, ORB)
            return carry

        lax.fori_loop(0, HALF // 2, scr_step, 0)

        def scr_part(k):
            return scr[:, rows_of(k), :].reshape(ROWS * ROWS, ORB)

        def scr_out_step(p, carry):
            first, second = exchange(scr_part(2 * p), scr_part(2 * p + 1))
            scr_out[h, 2 * p] = first
            scr_out[h, 2 * p + 1] = second
            return carry

        lax.fori_loop(0, GROUPS // 2, scr_out_step, 0)
        scr_in[:, pl.ds(my_share + h * HALF, HALF), :] = scr_out[h, 0]
        for k in range(1, GROUPS):
            scr_copy(h, k).start()

    for h in range(2):
        for k in range(1, GROUPS):
            scr_copy(h, k).wait_recv()

    def sig_step(p, carry):
        scr_spec = forward(fwd_l, scr_in, p)
        a_cos, a_sin = spec[p, :FREQ, :], spec[p, FREQ:, :]
        b_cos, b_sin = scr_spec[:FREQ], scr_spec[FREQ:]
        backward(inv_e, a_cos * b_cos - a_sin * b_sin, a_cos * b_sin + a_sin * b_cos, p, sig)
        return carry

    lax.fori_loop(0, PAIRS, sig_step, 0)

    low, high = to_share(sig, 0)
    sig_in[0:HALF, my_rows, :] = low
    sig_in[HALF:SHARE, my_rows, :] = high

    def sig_copy(k):
        return pltpu.make_async_remote_copy(
            src_ref=sig_out.at[k], dst_ref=sig_in.at[:, my_rows, :],
            send_sem=sig_s.at[k], recv_sem=sig_r.at[k],
            device_id={"energy": peer(me, k, 1)}, device_id_type=MESH,
        )

    def sig_out_step(k, carry):
        low, high = to_share(sig, k)
        sig_out[k, 0:HALF] = low
        sig_out[k, HALF:SHARE] = high
        return carry

    lax.fori_loop(1, GROUPS, sig_out_step, 0)
    for k in range(1, GROUPS):
        sig_copy(k).start()

    for k in range(1, GROUPS):
        less_copy(k).wait_send()
        for c in range(CHUNKS):
            great_copy(c, k).wait_send()
        for h in range(2):
            pol_copy(h, k).wait_send()
            scr_copy(h, k).wait_send()

    for h in range(2):
        for k in range(GROUPS):

            @pl.when(has_after)
            def _():
                near_copy(h, 0, k).wait_send()

            @pl.when(has_before)
            def _():
                near_copy(h, 1, k).wait_send()

    for k in range(1, GROUPS):
        sig_copy(k).wait_recv()
    store = pltpu.make_async_copy(sig_in, out_hbm, store_sem)
    store.start()
    for k in range(1, GROUPS):
        sig_copy(k).wait_send()
    store.wait()


def shards(g_less, g_great, coupling, coupling_mask):
    energy, lag = tables()
    any_space = pl.BlockSpec(memory_space=pl.ANY)
    vmem = pl.BlockSpec(memory_space=pltpu.VMEM)
    share = (SHARE, ORB, ORB)
    group = (ROWS, NE, ORB)
    to_rows = (GROUPS, ROWS, SHARE, ORB)
    dma = pltpu.SemaphoreType.DMA
    sigma = pl.pallas_call(
        kernel,
        out_shape=jax.ShapeDtypeStruct(share, BF16),
        in_specs=[any_space, any_space, vmem, pl.BlockSpec(memory_space=pltpu.SMEM)] + [any_space] * 5,
        out_specs=any_space,
        scratch_shapes=[
            pltpu.VMEM(share, BF16),
            pltpu.VMEM(share, BF16),
            pltpu.VMEM((2, PERIOD, NE), BF16),
            pltpu.VMEM((2, PERIOD, NE), BF16),
            pltpu.VMEM((2, NE, PERIOD), BF16),
            pltpu.VMEM((2, NE, PERIOD), BF16),
            pltpu.VMEM((NE, NE), BF16),
            pltpu.VMEM(to_rows, BF16),
            pltpu.VMEM(to_rows, BF16),
            pltpu.VMEM(group, BF16),
            pltpu.VMEM(group, BF16),
            pltpu.VMEM((PAIRS, PERIOD, 2 * ORB), F32),
            pltpu.VMEM(group, BF16),
            pltpu.VMEM((2, GROUPS, HALF, ROWS, ORB), BF16),
            pltpu.VMEM((2, HALF, ORB, ORB), BF16),
            pltpu.VMEM((2, 2, HALF, ORB, ORB), BF16),
            pltpu.VMEM(share, BF16),
            pltpu.VMEM((3, HALF, ORB, ORB), BF16),
            pltpu.VMEM((HALF, ORB, ORB), BF16),
            pltpu.VMEM((2, GROUPS, ROWS, HALF, ORB), BF16),
            pltpu.VMEM(group, BF16),
            pltpu.VMEM(group, BF16),
            pltpu.VMEM((GROUPS, SHARE, ROWS, ORB), BF16),
            pltpu.VMEM(share, BF16),
            dma((7,)),
            dma,
            dma((GROUPS,)), dma((GROUPS,)),
            dma((CHUNKS, GROUPS)), dma((CHUNKS, GROUPS)),
            dma((2, GROUPS)), dma((2, GROUPS)),
            dma((2, 2, GROUPS)), dma((2, 2, GROUPS)),
            dma((2, GROUPS)), dma((2, GROUPS)),
            dma((GROUPS,)), dma((GROUPS,)),
        ],
        compiler_params=pltpu.CompilerParams(
            collective_id=0, has_side_effects=True, vmem_limit_bytes=56 * 1024 * 1024
        ),
        name="gw",
    )(
        g_less, g_great, coupling, coupling_mask,
        jnp.asarray(energy), jnp.asarray(lag),
        jnp.asarray(np.ascontiguousarray(lag.transpose(0, 2, 1))),
        jnp.asarray(np.ascontiguousarray(energy.transpose(0, 2, 1))),
        jnp.asarray(swap_matrix()),
    )
    return sigma.astype(F32)[:, None]


def solution(mesh):
    return jax.shard_map(
        shards,
        mesh=mesh,
        in_specs=(
            P("energy", "block", None, None),
            P("energy", "block", None, None),
            P("block", None, None, None),
            P("block", None),
        ),
        out_specs=P("energy", "block", None, None),
        check_vma=False,
    )
```

time: 282 us -> 108 us (0.38)
  the two profiles are of different devices: /device:TPU:128 before, /device:TPU:8 now
where the time goes in v1:
time: 108 us; the launch traced here: 107 us
  Pallas kernels  104 us (96%)
  other arithmetic  2.79 us (3%)
    pallas_call x1, Pallas kernels, shards(): pl.pallas_call(kernel, out_shape=jax.ShapeDtypeStruct(share, BF16), in_sp...  104 us
    broadcast_in_dim x1, other arithmetic, shards(): return sigma.astype(F32)[:, None]  2.79 us

profile of v1, /device:TPU:8, one launch (start us, length us, event | category | flops | bytes accessed | tf_op | source)
XLA Modules:
  0.0 106.7 jit_solution(429202831306800275)
XLA Ops:
  0.0 103.9 %gw.1 = bf16[32,128,128]{2,1,0:T(8,128)(2,1)} custom-call(bf16[32,1,128,128]{3,2,1,0:T(8,128)(2,1)} %less_hbm.1, bf16[32,1,128,128]{3,2,1,0:T(8,128)(2,1)} %great_hbm.1, bf16[1,3,128,128]{3,2,1,0:T(8,128)(2,1)} %coupling_ref.1, s32[1,2]{1,0:T(1,128)} %mask_ref.1, bf16[2,384,256]{2,1,0:T(8,128)(2,1)} %constant.10.clone.fwd_e_hbm, ...), custom_call_target="tpu_custom_call" | custom-call | tf_op jit(solution)/shard_map/gw/pallas_call | solution.py:409
  103.9 2.8 %bitcast_convert_fusion = f32[32,1,128,128]{3,2,1,0:T(8,128)} fusion(bf16[32,128,128]{2,1,0:T(8,128)(2,1)} %gw.1), kind=kLoop, calls=%fused_computation | loop fusion | flops 524288 | bytes 3145728 | tf_op jit(solution)/shard_map/broadcast_in_dim | solution.py:459
